TPU v7x, 256 devices: a whole 4x4x8 slice. The times are simulated.
256 devices in a mesh: star: 8 (over x, core), row: 32 (over z, y).
Axes of the slice: x: 4, y: 4, z: 8, core: 2. Of those that a mesh axis runs over, the one named last changes fastest.
Arguments:
- feature_maps: bfloat16 [64, 1024, 1024], P(None, 'row'), may hold values from -6 to 6
- coef_table: bfloat16 [64, 64], replicated, may hold values from -0.119628906 to 0.119628906
- star_counts: int32 [8], replicated, may hold values from 1 to 12, 32 in all
- star_cells: int32 [8, 12], replicated, may hold values from 0 to 63
- star_bands: int32 [8, 12], replicated, may hold values from 0 to 7
- psf_cotangent: bfloat16 [96, 1024, 1024], P('star', 'row'), may hold values from -6 to 6
Outputs:
- map_grad: float32 [64, 1024, 1024], P('star', 'row')
- coef_grad: float32 [64, 64], replicated
Inputs may be any that keep to these rules, and one draw needn't show every extreme that they name: The live stars of group g fill its slots 0 to star_counts[g] - 1; the counts sum to 32, and some group has exactly 12.
All inputs are finite; a program needn't handle non-finite values.
Results may differ from a plain program's by a relative error of at most 0.008.
Values may be sent and summed in bfloat16 or wider, within the bound.
No kernel may reach another device: no remote copies, remote signals or barrier semaphores. Data moves between devices by JAX's collectives and lax.ppermute only.
A program may use at most 128 MiB of HBM per device.

v0:
```python
import jax
import jax.numpy as jnp
from jax import lax
from jax.sharding import PartitionSpec as P

BANDS = 8


def fourier_tables(pupil_size):
    index_row = jnp.arange(pupil_size, dtype=jnp.int32)
    products = index_row[:, None] * index_row[None, :] % pupil_size
    angles = 2.0 * jnp.pi / pupil_size * products.astype(jnp.float32)
    return (jnp.cos(angles).astype(jnp.bfloat16), (-jnp.sin(angles)).astype(jnp.bfloat16))


def aperture_rows(first_row, row_count, pupil_size):
    centre = 0.5 * (pupil_size - 1)
    row_pos = (first_row + jnp.arange(row_count, dtype=jnp.int32)).astype(jnp.float32) - centre
    col_pos = jnp.arange(pupil_size, dtype=jnp.int32).astype(jnp.float32) - centre
    radius = row_pos[:, None] * row_pos[:, None] + col_pos[None, :] * col_pos[None, :]
    return jnp.where(radius <= 0.25 * pupil_size * pupil_size, 1.0, 0.0).astype(jnp.float32)


def wave_numbers(band_ids):
    wavelength = 0.55 + 0.35 * band_ids.astype(jnp.float32) / (BANDS - 1)
    return 2.0 * jnp.pi / wavelength


def table_pick(values, indices):
    positions = jnp.arange(values.shape[0], dtype=jnp.int32)
    chosen = jnp.where(positions[None, :] == indices[:, None], values[None, :], 0)
    return jnp.sum(chosen, axis=1)


def per_device(feature_maps, coef_table, star_counts, star_cells, star_bands, psf_cotangent):
    groups = lax.axis_size("star")
    my_group = lax.axis_index("star")
    slot_count = psf_cotangent.shape[0]
    map_count, row_count, pupil_size = feature_maps.shape
    flat_cells = star_cells.reshape(-1)
    flat_bands = star_bands.reshape(-1)
    cell_count = coef_table.shape[0]
    within = jnp.arange(slot_count, dtype=jnp.int32)
    owner_group = jnp.zeros_like(within) + my_group
    live_mask = within < table_pick(star_counts, owner_group)
    owner_group, within, live_mask = (owner_group, within, live_mask)
    slot_index = owner_group * slot_count + within
    cell_ids = table_pick(flat_cells, slot_index)
    band_ids = table_pick(flat_bands, slot_index)
    cell_hot = cell_ids[:, None] == jnp.arange(cell_count, dtype=jnp.int32)[None, :]
    coef_rows = jnp.dot(
        cell_hot.astype(jnp.bfloat16), coef_table, preferred_element_type=jnp.float32
    ).astype(jnp.bfloat16)
    flat_maps = feature_maps.reshape(map_count, row_count * pupil_size)
    path_error = jnp.dot(coef_rows, flat_maps, preferred_element_type=jnp.float32).reshape(
        -1, row_count, pupil_size
    )
    wave_number = wave_numbers(band_ids)
    phase_angle = wave_number[:, None, None] * path_error
    aperture = aperture_rows(lax.axis_index("row") * row_count, row_count, pupil_size)
    cos_phase = jnp.cos(phase_angle)
    sin_phase = jnp.sin(phase_angle)
    pupil_field = jnp.stack([aperture * cos_phase, aperture * sin_phase], 1).astype(jnp.bfloat16)
    cos_table, sin_table = fourier_tables(pupil_size)
    inverse = 1.0 / pupil_size
    along_cos = jnp.einsum(
        "sarc,cv->sarv", pupil_field, cos_table, preferred_element_type=jnp.float32
    )
    along_sin = jnp.einsum(
        "sarc,cv->sarv", pupil_field, sin_table, preferred_element_type=jnp.float32
    )
    column_field = jnp.stack(
        [along_cos[:, 0] - along_sin[:, 1], along_sin[:, 0] + along_cos[:, 1]], 1
    ).astype(jnp.bfloat16)
    pieces = lax.all_to_all(column_field, "row", split_axis=3, concat_axis=2, tiled=True)
    row_cos = jnp.einsum("sarv,ru->savu", pieces, cos_table, preferred_element_type=jnp.float32)
    row_sin = jnp.einsum("sarv,ru->savu", pieces, sin_table, preferred_element_type=jnp.float32)
    real_part = (row_cos[:, 0] - row_sin[:, 1]) * inverse
    imag_part = (row_sin[:, 0] + row_cos[:, 1]) * inverse
    focal_field = jnp.stack([real_part, imag_part], 1)
    weight = jnp.where(live_mask, 2.0, 0.0).astype(jnp.float32)[:, None, None, None]
    focal_grad = (weight * psf_cotangent.astype(jnp.float32)[:, None] * focal_field).astype(
        jnp.bfloat16
    )
    back_cos = jnp.einsum(
        "savu,ur->savr", focal_grad, cos_table, preferred_element_type=jnp.float32
    )
    back_sin = jnp.einsum(
        "savu,ur->savr", focal_grad, sin_table, preferred_element_type=jnp.float32
    )
    spectrum_grad = jnp.stack(
        [(back_cos[:, 0] + back_sin[:, 1]) * inverse, (back_cos[:, 1] - back_sin[:, 0]) * inverse],
        1,
    ).astype(jnp.bfloat16)
    pieces = lax.all_to_all(spectrum_grad, "row", split_axis=3, concat_axis=2, tiled=True)
    col_cos = jnp.einsum("savr,vc->sarc", pieces, cos_table, preferred_element_type=jnp.float32)
    col_sin = jnp.einsum("savr,vc->sarc", pieces, sin_table, preferred_element_type=jnp.float32)
    pupil_grad = jnp.stack([col_cos[:, 0] + col_sin[:, 1], col_cos[:, 1] - col_sin[:, 0]], 1)
    phase_grad = aperture * (cos_phase * pupil_grad[:, 1] - sin_phase * pupil_grad[:, 0])
    path_grad = (
        (wave_number[:, None, None] * phase_grad)
        .astype(jnp.bfloat16)
        .reshape(-1, row_count * pupil_size)
    )
    map_scores = lax.dot_general(
        path_grad, flat_maps, (((1,), (1,)), ((), ())), preferred_element_type=jnp.float32
    )
    coef_part = lax.dot_general(
        cell_hot.astype(jnp.float32),
        map_scores * (1.0 / (8 * pupil_size)),
        (((0,), (0,)), ((), ())),
        precision=lax.Precision.HIGHEST,
    )
    coef_grad = lax.psum(coef_part, ("star", "row"))
    share = map_count // groups
    map_grad = lax.psum_scatter(
        lax.dot_general(
            coef_rows, path_grad, (((0,), (0,)), ((), ())), preferred_element_type=jnp.float32
        ),
        "star",
        scatter_dimension=0,
        tiled=True,
    )
    return (map_grad.reshape(share, row_count, pupil_size), coef_grad)


def solution(mesh):
    placed = (P(None, "row", None), P(), P(), P(), P(), P("star", "row", None))
    return jax.shard_map(
        per_device,
        mesh=mesh,
        in_specs=placed,
        out_specs=(P("star", "row", None), P()),
        check_vma=False,
    )
```

profile of v0, /device:TPU:1, one launch (start us, length us, event | category | flops | bytes accessed | tf_op | source)
XLA Modules:
  0.0 501.8 jit_solution(5607141360308045111)
XLA Ops:
  16.0 8.4 %fusion.54 = (bf16[12,1,32,1024]{3,0,2,1:T(8,128)(2,1)S(1)}, bf16[12,1,32,1024]{3,0,2,1:T(8,128)(2,1)S(1)}) fusion(f32[12,32,1024]{2,0,1:T(8,128)S(1)} %fusion.3, f32[32,1024]{1,0:T(8,128)S(1)} %fusion.56, f32[12]{0:T(128)S(1)} %add_divide_fusion), kind=kLoop, calls=%fused_computation.67 | loop fusion | flops 1966080 | bytes 3276848 | tf_op jit(solution)/shard_map/stack | solution.py:63
  24.7 17.9 %fusion.28 = f32[12,2,32,1024]{3,2,1,0:T(8,128)S(1)} fusion(bf16[12,2,32,1024]{3,0,2,1:T(8,128)(2,1)S(1)} %pad_maximum_fusion), kind=kOutput, calls=%fused_computation.36 | convolution fusion | flops 1627389952 | bytes 4718592 | tf_op jit(solution)/shard_map/sarc,cv->sarv/dot_general | solution.py:69
  42.5 17.3 %fusion.36 = f32[12,2,32,1024]{3,2,1,0:T(8,128)S(1)} fusion(bf16[12,2,32,1024]{3,0,2,1:T(8,128)(2,1)S(1)} %pad_maximum_fusion), kind=kOutput, calls=%fused_computation.40 | convolution fusion | flops 1626341376 | bytes 4718592 | tf_op jit(solution)/shard_map/sarc,cv->sarv/dot_general | solution.py:66
  62.4 15.1 %copy.45 = bf16[12,2,32,1024]{2,1,0,3:T(2,128)(2,1)} copy(bf16[12,2,32,1024]{3,2,1,0:T(8,128)(2,1)} %pad_maximum_fusion.1) | data formatting | bytes 3145728 | tf_op jit(solution)/shard_map/stack | solution.py:72
  77.5 13.8 %reshape.93 = bf16[32,2,12288]{2,1,0:T(2,128)(2,1)} reshape(bf16[1024,12,2,32]{3,2,1,0:T(2,128)(2,1)} %bitcast.93) | data formatting | bytes 3145728
  91.3 12.3 %all-to-all-start = ((bf16[32,2,12288]{2,1,0:T(2,128)(2,1)}), bf16[32,2,12288]{2,1,0:T(2,128)(2,1)}, u32[]{:S(2)}, u32[]{:S(2)}) async-start(bf16[32,2,12288]{2,1,0:T(2,128)(2,1)} %reshape.93), calls=%async_computation | async-start | bytes 3145728 | tf_op jit(solution)/shard_map/all_to_all | solution.py:75
  105.2 36.3 %all-to-all-done = bf16[32,2,12288]{2,1,0:T(2,128)(2,1)} async-done(((bf16[32,2,12288]{2,1,0:T(2,128)(2,1)}), bf16[32,2,12288]{2,1,0:T(2,128)(2,1)}, u32[]{:S(2)}, u32[]{:S(2)}) %all-to-all-start) | async-done | bytes 1572896 | tf_op jit(solution)/shard_map/all_to_all | solution.py:75
  141.5 14.3 %reshape.94 = bf16[1024,12,2,32]{3,2,1,0:T(2,128)(2,1)} reshape(bf16[32,2,12288]{2,1,0:T(2,128)(2,1)} %all-to-all-done) | data formatting | bytes 3145728
  155.7 9.5 %copy.107 = bf16[12,2,32,32,32]{2,3,4,1,0:T(8,128)(2,1)} copy(bf16[12,2,32,32,32]{2,1,0,4,3:T(2,128)(2,1)} %bitcast.89) | data formatting | bytes 3145728 | tf_op jit(solution)/shard_map/all_to_all | solution.py:75
  165.2 9.8 %all_to_all.29 = bf16[12,2,1024,32]{2,3,1,0:T(8,128)(2,1)} reshape(bf16[12,2,32,32,32]{3,2,4,1,0:T(8,128)(2,1)} %bitcast.90) | data formatting | bytes 3145728 | tf_op jit(solution)/shard_map/all_to_all | solution.py:75
  175.0 18.3 %fusion.26 = f32[12,2,32,1024]{3,2,1,0:T(8,128)S(1)} fusion(bf16[12,2,1024,32]{2,3,1,0:T(8,128)(2,1)} %all_to_all.29), kind=kOutput, calls=%fused_computation.35 | convolution fusion | flops 1627389952 | bytes 4718592 | tf_op jit(solution)/shard_map/sarv,ru->savu/dot_general | solution.py:77
  193.3 17.4 %fusion.34 = f32[12,2,32,1024]{3,2,1,0:T(8,128)S(1)} fusion(bf16[12,2,1024,32]{2,3,1,0:T(8,128)(2,1)S(1)} %copy-done.3), kind=kOutput, calls=%fused_computation.39 | convolution fusion | flops 1626341376 | bytes 4718592 | tf_op jit(solution)/shard_map/sarv,ru->savu/dot_general | solution.py:76
  212.1 16.4 %fusion.32 = f32[12,2,32,1024]{3,2,1,0:T(8,128)S(1)} fusion(f32[12,1,32,1024]{3,2,1,0:T(8,128)S(1)} %get-tuple-element.15, f32[12,1,32,1024]{3,2,1,0:T(8,128)S(1)} %get-tuple-element.14, f32[12,32,1024]{2,1,0:T(8,128)S(1)} %copy-done.2), kind=kOutput, calls=%fused_computation.38 | convolution fusion | flops 1628700672 | bytes 7864320 | tf_op jit(solution)/shard_map/savu,ur->savr/dot_general | solution.py:85
  228.5 16.7 %fusion.24 = f32[12,2,32,1024]{3,2,1,0:T(8,128)S(1)} fusion(f32[12,1,32,1024]{3,2,1,0:T(8,128)S(1)} %get-tuple-element.15, f32[12,1,32,1024]{3,2,1,0:T(8,128)S(1)} %get-tuple-element.14, f32[12,32,1024]{2,1,0:T(8,128)S(1)} %copy-done.2), kind=kOutput, calls=%fused_computation.34 | convolution fusion | flops 1629749248 | bytes 7864320 | tf_op jit(solution)/shard_map/savu,ur->savr/dot_general | solution.py:88
  247.2 15.1 %copy.47 = bf16[12,2,32,1024]{2,1,0,3:T(2,128)(2,1)} copy(bf16[12,2,32,1024]{3,2,1,0:T(8,128)(2,1)} %pad_maximum_fusion.2) | data formatting | bytes 3145728 | tf_op jit(solution)/shard_map/stack | solution.py:91
  262.3 14.2 %reshape.95 = bf16[32,2,12288]{2,1,0:T(2,128)(2,1)} reshape(bf16[1024,12,2,32]{3,2,1,0:T(2,128)(2,1)} %bitcast.94) | data formatting | bytes 3145728
  276.5 42.9 %all_to_all.36 = bf16[32,2,12288]{2,1,0:T(2,128)(2,1)} all-to-all(bf16[32,2,12288]{2,1,0:T(2,128)(2,1)} %reshape.95), channel_id=1, replica_groups=mesh['star'=8,'row'=32] {'row'}, dimensions={0} | all-to-all | bytes 3145728 | tf_op jit(solution)/shard_map/all_to_all | solution.py:95
  319.5 14.3 %reshape.96 = bf16[1024,12,2,32]{3,2,1,0:T(2,128)(2,1)} reshape(bf16[32,2,12288]{2,1,0:T(2,128)(2,1)} %all_to_all.36) | data formatting | bytes 3145728
  333.7 9.5 %copy.106 = bf16[12,2,32,32,32]{2,3,4,1,0:T(8,128)(2,1)} copy(bf16[12,2,32,32,32]{2,1,0,4,3:T(2,128)(2,1)} %bitcast.91) | data formatting | bytes 3145728 | tf_op jit(solution)/shard_map/all_to_all | solution.py:95
  343.2 9.8 %all_to_all.33 = bf16[12,2,1024,32]{2,3,1,0:T(8,128)(2,1)} reshape(bf16[12,2,32,32,32]{3,2,4,1,0:T(8,128)(2,1)} %bitcast.92) | data formatting | bytes 3145728 | tf_op jit(solution)/shard_map/all_to_all | solution.py:95
  353.0 18.3 %fusion.22 = f32[12,2,32,1024]{3,2,1,0:T(8,128)S(1)} fusion(bf16[12,2,1024,32]{2,3,1,0:T(8,128)(2,1)} %all_to_all.33), kind=kOutput, calls=%fused_computation.33 | convolution fusion | flops 1627389952 | bytes 4718592 | tf_op jit(solution)/shard_map/savr,vc->sarc/dot_general | solution.py:97
  371.3 17.0 %fusion.30 = f32[12,2,32,1024]{3,2,1,0:T(8,128)S(1)} fusion(bf16[12,2,1024,32]{2,3,1,0:T(8,128)(2,1)S(1)} %copy-done.4), kind=kOutput, calls=%fused_computation.37 | convolution fusion | flops 1626341376 | bytes 4718592 | tf_op jit(solution)/shard_map/savr,vc->sarc/dot_general | solution.py:96
  389.4 11.4 %fusion.19 = bf16[12,32,1024]{2,0,1:T(8,128)(2,1)S(1)} fusion(f32[12,1,32,1024]{3,2,1,0:T(8,128)S(1)} %get-tuple-element.24, f32[12,1,32,1024]{3,2,1,0:T(8,128)S(1)} %get-tuple-element.19, f32[12,1,32,1024]{3,2,1,0:T(8,128)S(1)} %get-tuple-element.25, f32[12,1,32,1024]{3,2,1,0:T(8,128)S(1)} %get-tuple-element.18, f32[12,32,1024]{2,0,1:T(8,128)S(1)} %fusion.3, ...), kind=kLoop, calls=%fused_computation.29 | loop fusion | flops 3538944 | bytes 8781872 | tf_op jit(solution)/shard_map/convert_element_type | solution.py:102
  413.6 78.1 %psum.7 = f32[64,64]{1,0:T(8,128)} all-reduce(f32[64,64]{1,0:T(8,128)S(1)} %fusion.57), channel_id=1, replica_groups=mesh['star'=8,'row'=32] {'star','row'}, use_global_device_ids=true, to_apply=%region_4.5 | all-reduce | flops 4096 | bytes 32768 | tf_op jit(solution)/shard_map/psum | solution.py:114
  (44 shorter events, 33.2 us)
Async XLA Ops:
  7.2 1.8 copy-start
  91.3 12.3 %copy-start.6 = (s32[8]{0:T(128)S(1)}, s32[8]{0:T(128)}, u32[]{:S(2)}) copy-start(s32[8]{0:T(128)} %param.8) | copy-start | bytes 100
  91.3 12.4 %copy-start.5 = (bf16[12,32,1024]{2,1,0:T(8,128)(2,1)S(1)}, bf16[12,32,1024]{2,1,0:T(8,128)(2,1)}, u32[]{:S(2)}) copy-start(bf16[12,32,1024]{2,1,0:T(8,128)(2,1)} %param.11) | copy-start | bytes 2359300
  91.3 50.2 %all-to-all-start = ((bf16[32,2,12288]{2,1,0:T(2,128)(2,1)}), bf16[32,2,12288]{2,1,0:T(2,128)(2,1)}, u32[]{:S(2)}, u32[]{:S(2)}) async-start(bf16[32,2,12288]{2,1,0:T(2,128)(2,1)} %reshape.93), calls=%async_computation | async-start | bytes 3145728 | tf_op jit(solution)/shard_map/all_to_all | solution.py:75
  103.6 388.1 %reduce-scatter.2.cloned.1.call-start = ((), (), s32[]{:S(2)}) async-start(), calls=%async_computation.3 | async-start | bytes 9437184 | tf_op jit(solution)/shard_map/reduce_scatter | solution.py:116
  175.0 18.3 %copy-start.3 = (bf16[12,2,1024,32]{2,3,1,0:T(8,128)(2,1)S(1)}, bf16[12,2,1024,32]{2,3,1,0:T(8,128)(2,1)}, u32[]{:S(2)}) copy-start(bf16[12,2,1024,32]{2,3,1,0:T(8,128)(2,1)} %all_to_all.29) | copy-start | bytes 4718596
  210.7 1.4 copy-start.2
  353.0 18.3 %copy-start.4 = (bf16[12,2,1024,32]{2,3,1,0:T(8,128)(2,1)S(1)}, bf16[12,2,1024,32]{2,3,1,0:T(8,128)(2,1)}, u32[]{:S(2)}) copy-start(bf16[12,2,1024,32]{2,3,1,0:T(8,128)(2,1)} %all_to_all.33) | copy-start | bytes 4718596
  406.5 88.0 %copy-start.1 = (bf16[64,64]{1,0:T(8,128)(2,1)S(1)}, bf16[64,64]{1,0:T(8,128)(2,1)}, u32[]{:S(2)}) copy-start(bf16[64,64]{1,0:T(8,128)(2,1)} %param.7) | copy-start | bytes 24580
Sparse Core Ops, SparseCore 0:
  406.6 54.6 reduce-scatter.1
where the time goes:
time: 509 us; the launch traced here: 502 us
  matrix products  158 us (31%)
  local copies, waits for them, and re-layouts  132 us (26%)
  blocking collectives  121 us (24%)
  waiting for transfers between devices  36.3 us (7%)
  other arithmetic  27.5 us (5%)
  between operations  14.7 us (3%)
  starting transfers between devices  12.3 us (2%)
    psum x1, blocking collectives, per_device(): coef_grad = lax.psum(coef_part, ('star', 'row'))  78.1 us
    unnamed x21, local copies, waits for them, and re-layouts  60.5 us
    all_to_all x1, blocking collectives, per_device(): lax.all_to_all(spectrum_grad, 'row', split_axis=3, concat_axis=2, tiled=T...  42.9 us
    all_to_all x1, waiting for transfers between devices, per_device(): lax.all_to_all(column_field, 'row', split_axis=3, concat_axis=2, tiled=True)  36.3 us
    all_to_all x2, local copies, waits for them, and re-layouts, per_device(): lax.all_to_all(column_field, 'row', split_axis=3, concat_axis=2, tiled=True)  19.3 us
    all_to_all x2, local copies, waits for them, and re-layouts, per_device(): lax.all_to_all(spectrum_grad, 'row', split_axis=3, concat_axis=2, tiled=T...  19.3 us
    dot_general x1, matrix products, per_device(): jnp.einsum('savr,vc->sarc', pieces, sin_table, preferred_element_type=jnp...  18.3 us
    dot_general x1, matrix products, per_device(): jnp.einsum('sarv,ru->savu', pieces, sin_table, preferred_element_type=jnp...  18.3 us
  transfers between devices with their start and end apart: 2, of which 1 were waited for; matrix products, arithmetic and copies ran while one was open for 2% of the time, Pallas kernels for 0%

commit v1 on v0

--- a/solution.py
+++ b/solution.py
@@ -111,7 +111,7 @@
         (((0,), (0,)), ((), ())),
         precision=lax.Precision.HIGHEST,
     )
-    coef_grad = lax.psum(coef_part, ("star", "row"))
+    coef_grad = jnp.sum(lax.all_gather(coef_part, ("star", "row")), axis=0)
     share = map_count // groups
     map_grad = lax.psum_scatter(
         lax.dot_general(

time: 509 us -> 552 us (1.084)
  waiting for transfers between devices: 36.3 us -> 152 us
  blocking collectives: 121 us -> 42.9 us
    all_gather x0 -> x1, waiting for transfers between devices: none -> 116 us  [per_device(): coef_grad = jnp.sum(lax.all_gather(coef_part, ('star', 'row')), axis=0)]
    psum x1 -> x0, blocking collectives: 78.1 us -> none  [per_device(): coef_grad = lax.psum(coef_part, ('star', 'row'))]
    unnamed x21 -> x23, local copies, waits for them, and re-layouts: 60.5 us -> 60.5 us
  transfers between devices with their start and end apart: 2 -> 3, of which waited for: 1 -> 2; matrix products, arithmetic and copies ran while one was open for 2% -> 2% of each run, Pallas kernels for 0% -> 0%
where the time goes in v1:
time: 552 us; the launch traced here: 544 us
  matrix products  156 us (28%)
  waiting for transfers between devices  152 us (28%)
  local copies, waits for them, and re-layouts  132 us (24%)
  blocking collectives  42.9 us (8%)
  other arithmetic  32.1 us (6%)
  between operations  16.2 us (3%)
  starting transfers between devices  12.4 us (2%)
    all_gather x1, waiting for transfers between devices, per_device(): coef_grad = jnp.sum(lax.all_gather(coef_part, ('star', 'row')), axis=0)  116 us
    unnamed x23, local copies, waits for them, and re-layouts  60.5 us
    all_to_all x1, blocking collectives, per_device(): lax.all_to_all(spectrum_grad, 'row', split_axis=3, concat_axis=2, tiled=T...  42.9 us
    all_to_all x1, waiting for transfers between devices, per_device(): lax.all_to_all(column_field, 'row', split_axis=3, concat_axis=2, tiled=True)  36.3 us
    all_to_all x2, local copies, waits for them, and re-layouts, per_device(): lax.all_to_all(column_field, 'row', split_axis=3, concat_axis=2, tiled=True)  19.2 us
    all_to_all x2, local copies, waits for them, and re-layouts, per_device(): lax.all_to_all(spectrum_grad, 'row', split_axis=3, concat_axis=2, tiled=T...  19.2 us
    dot_general x1, matrix products, per_device(): jnp.einsum('savr,vc->sarc', pieces, sin_table, preferred_element_type=jnp...  18.3 us
    dot_general x1, matrix products, per_device(): jnp.einsum('sarv,ru->savu', pieces, sin_table, preferred_element_type=jnp...  18.3 us
  transfers between devices with their start and end apart: 3, of which 2 were waited for; matrix products, arithmetic and copies ran while one was open for 2% of the time, Pallas kernels for 0%

profile of v1, /device:TPU:1, one launch (start us, length us, event | category | flops | bytes accessed | tf_op | source)
XLA Modules:
  0.0 544.1 jit_solution(18122331977936464397)
XLA Ops:
  16.8 8.4 %fusion.54 = (bf16[12,1,32,1024]{3,0,2,1:T(8,128)(2,1)S(1)}, bf16[12,1,32,1024]{3,0,2,1:T(8,128)(2,1)S(1)}) fusion(f32[12,32,1024]{2,0,1:T(8,128)S(1)} %fusion.3, f32[32,1024]{1,0:T(8,128)S(1)} %fusion.56, f32[12]{0:T(128)S(1)} %add_divide_fusion), kind=kLoop, calls=%fused_computation.67 | loop fusion | flops 1966080 | bytes 3276848 | tf_op jit(solution)/shard_map/stack | solution.py:63
  25.5 17.9 %fusion.28 = f32[12,2,32,1024]{3,2,1,0:T(8,128)S(1)} fusion(bf16[12,2,32,1024]{3,0,2,1:T(8,128)(2,1)S(1)} %pad_maximum_fusion), kind=kOutput, calls=%fused_computation.36 | convolution fusion | flops 1627389952 | bytes 4718592 | tf_op jit(solution)/shard_map/sarc,cv->sarv/dot_general | solution.py:69
  43.4 17.3 %fusion.36 = f32[12,2,32,1024]{3,2,1,0:T(8,128)S(1)} fusion(bf16[12,2,32,1024]{3,0,2,1:T(8,128)(2,1)S(1)} %pad_maximum_fusion), kind=kOutput, calls=%fused_computation.40 | convolution fusion | flops 1626341376 | bytes 4718592 | tf_op jit(solution)/shard_map/sarc,cv->sarv/dot_general | solution.py:66
  63.2 15.0 %copy.45 = bf16[12,2,32,1024]{2,1,0,3:T(2,128)(2,1)} copy(bf16[12,2,32,1024]{3,2,1,0:T(8,128)(2,1)} %pad_maximum_fusion.1) | data formatting | bytes 3145728 | tf_op jit(solution)/shard_map/stack | solution.py:72
  78.3 13.8 %reshape.94 = bf16[32,2,12288]{2,1,0:T(2,128)(2,1)} reshape(bf16[1024,12,2,32]{3,2,1,0:T(2,128)(2,1)} %bitcast.94) | data formatting | bytes 3145728
  92.1 12.3 %all-to-all-start = ((bf16[32,2,12288]{2,1,0:T(2,128)(2,1)}), bf16[32,2,12288]{2,1,0:T(2,128)(2,1)}, u32[]{:S(2)}, u32[]{:S(2)}) async-start(bf16[32,2,12288]{2,1,0:T(2,128)(2,1)} %reshape.94), calls=%async_computation | async-start | bytes 3145728 | tf_op jit(solution)/shard_map/all_to_all | solution.py:75
  106.0 36.3 %all-to-all-done = bf16[32,2,12288]{2,1,0:T(2,128)(2,1)} async-done(((bf16[32,2,12288]{2,1,0:T(2,128)(2,1)}), bf16[32,2,12288]{2,1,0:T(2,128)(2,1)}, u32[]{:S(2)}, u32[]{:S(2)}) %all-to-all-start) | async-done | bytes 1572896 | tf_op jit(solution)/shard_map/all_to_all | solution.py:75
  142.3 14.3 %reshape.95 = bf16[1024,12,2,32]{3,2,1,0:T(2,128)(2,1)} reshape(bf16[32,2,12288]{2,1,0:T(2,128)(2,1)} %all-to-all-done) | data formatting | bytes 3145728
  156.5 9.5 %copy.107 = bf16[12,2,32,32,32]{2,3,4,1,0:T(8,128)(2,1)} copy(bf16[12,2,32,32,32]{2,1,0,4,3:T(2,128)(2,1)} %bitcast.90) | data formatting | bytes 3145728 | tf_op jit(solution)/shard_map/all_to_all | solution.py:75
  166.0 9.8 %all_to_all.29 = bf16[12,2,1024,32]{2,3,1,0:T(8,128)(2,1)} reshape(bf16[12,2,32,32,32]{3,2,4,1,0:T(8,128)(2,1)} %bitcast.91) | data formatting | bytes 3145728 | tf_op jit(solution)/shard_map/all_to_all | solution.py:75
  175.8 18.3 %fusion.26 = f32[12,2,32,1024]{3,2,1,0:T(8,128)S(1)} fusion(bf16[12,2,1024,32]{2,3,1,0:T(8,128)(2,1)} %all_to_all.29), kind=kOutput, calls=%fused_computation.35 | convolution fusion | flops 1627389952 | bytes 4718592 | tf_op jit(solution)/shard_map/sarv,ru->savu/dot_general | solution.py:77
  194.1 17.4 %fusion.34 = f32[12,2,32,1024]{3,2,1,0:T(8,128)S(1)} fusion(bf16[12,2,1024,32]{2,3,1,0:T(8,128)(2,1)S(1)} %copy-done.4), kind=kOutput, calls=%fused_computation.39 | convolution fusion | flops 1626341376 | bytes 4718592 | tf_op jit(solution)/shard_map/sarv,ru->savu/dot_general | solution.py:76
  212.9 16.4 %fusion.32 = f32[12,2,32,1024]{3,2,1,0:T(8,128)S(1)} fusion(f32[12,1,32,1024]{3,2,1,0:T(8,128)S(1)} %get-tuple-element.15, f32[12,1,32,1024]{3,2,1,0:T(8,128)S(1)} %get-tuple-element.14, f32[12,32,1024]{2,1,0:T(8,128)S(1)} %copy-done.3), kind=kOutput, calls=%fused_computation.38 | convolution fusion | flops 1628700672 | bytes 7864320 | tf_op jit(solution)/shard_map/savu,ur->savr/dot_general | solution.py:85
  229.3 16.7 %fusion.24 = f32[12,2,32,1024]{3,2,1,0:T(8,128)S(1)} fusion(f32[12,1,32,1024]{3,2,1,0:T(8,128)S(1)} %get-tuple-element.15, f32[12,1,32,1024]{3,2,1,0:T(8,128)S(1)} %get-tuple-element.14, f32[12,32,1024]{2,1,0:T(8,128)S(1)} %copy-done.3), kind=kOutput, calls=%fused_computation.34 | convolution fusion | flops 1629749248 | bytes 7864320 | tf_op jit(solution)/shard_map/savu,ur->savr/dot_general | solution.py:88
  248.0 15.0 %copy.47 = bf16[12,2,32,1024]{2,1,0,3:T(2,128)(2,1)} copy(bf16[12,2,32,1024]{3,2,1,0:T(8,128)(2,1)} %pad_maximum_fusion.2) | data formatting | bytes 3145728 | tf_op jit(solution)/shard_map/stack | solution.py:91
  263.1 14.2 %reshape.96 = bf16[32,2,12288]{2,1,0:T(2,128)(2,1)} reshape(bf16[1024,12,2,32]{3,2,1,0:T(2,128)(2,1)} %bitcast.95) | data formatting | bytes 3145728
  277.3 42.9 %all_to_all.36 = bf16[32,2,12288]{2,1,0:T(2,128)(2,1)} all-to-all(bf16[32,2,12288]{2,1,0:T(2,128)(2,1)} %reshape.96), channel_id=1, replica_groups=mesh['star'=8,'row'=32] {'row'}, dimensions={0} | all-to-all | bytes 3145728 | tf_op jit(solution)/shard_map/all_to_all | solution.py:95
  320.2 14.3 %reshape.97 = bf16[1024,12,2,32]{3,2,1,0:T(2,128)(2,1)} reshape(bf16[32,2,12288]{2,1,0:T(2,128)(2,1)} %all_to_all.36) | data formatting | bytes 3145728
  334.5 9.5 %copy.106 = bf16[12,2,32,32,32]{2,3,4,1,0:T(8,128)(2,1)} copy(bf16[12,2,32,32,32]{2,1,0,4,3:T(2,128)(2,1)} %bitcast.92) | data formatting | bytes 3145728 | tf_op jit(solution)/shard_map/all_to_all | solution.py:95
  343.9 9.8 %all_to_all.33 = bf16[12,2,1024,32]{2,3,1,0:T(8,128)(2,1)} reshape(bf16[12,2,32,32,32]{3,2,4,1,0:T(8,128)(2,1)} %bitcast.93) | data formatting | bytes 3145728 | tf_op jit(solution)/shard_map/all_to_all | solution.py:95
  353.7 18.3 %fusion.22 = f32[12,2,32,1024]{3,2,1,0:T(8,128)S(1)} fusion(bf16[12,2,1024,32]{2,3,1,0:T(8,128)(2,1)} %all_to_all.33), kind=kOutput, calls=%fused_computation.33 | convolution fusion | flops 1627389952 | bytes 4718592 | tf_op jit(solution)/shard_map/savr,vc->sarc/dot_general | solution.py:97
  372.0 17.0 %fusion.30 = f32[12,2,32,1024]{3,2,1,0:T(8,128)S(1)} fusion(bf16[12,2,1024,32]{2,3,1,0:T(8,128)(2,1)S(1)} %copy-done.5), kind=kOutput, calls=%fused_computation.37 | convolution fusion | flops 1626341376 | bytes 4718592 | tf_op jit(solution)/shard_map/savr,vc->sarc/dot_general | solution.py:96
  390.1 11.4 %fusion.19 = bf16[12,32,1024]{2,0,1:T(8,128)(2,1)S(1)} fusion(f32[12,1,32,1024]{3,2,1,0:T(8,128)S(1)} %get-tuple-element.24, f32[12,1,32,1024]{3,2,1,0:T(8,128)S(1)} %get-tuple-element.19, f32[12,1,32,1024]{3,2,1,0:T(8,128)S(1)} %get-tuple-element.25, f32[12,1,32,1024]{3,2,1,0:T(8,128)S(1)} %get-tuple-element.18, f32[12,32,1024]{2,0,1:T(8,128)S(1)} %fusion.3, ...), kind=kLoop, calls=%fused_computation.29 | loop fusion | flops 3538944 | bytes 8781872 | tf_op jit(solution)/shard_map/convert_element_type | solution.py:102
  412.8 116.0 %all-gather.3.cloned.1.call-done = f32[16384,64]{1,0:T(8,128)} async-done(((f32[64,64]{1,0:T(8,128)}), f32[16384,64]{1,0:T(8,128)}) %all-gather.3.cloned.1.call-update) | async-done | bytes 4194320 | tf_op jit(solution)/shard_map/all_gather | solution.py:114
  (49 shorter events, 36.3 us)
Async XLA Ops:
  8.0 1.8 copy-start
  92.1 12.3 %copy-start.7 = (s32[8]{0:T(128)S(1)}, s32[8]{0:T(128)}, u32[]{:S(2)}) copy-start(s32[8]{0:T(128)} %param.8) | copy-start | bytes 100
  92.1 12.4 %copy-start.6 = (bf16[12,32,1024]{2,1,0:T(8,128)(2,1)S(1)}, bf16[12,32,1024]{2,1,0:T(8,128)(2,1)}, u32[]{:S(2)}) copy-start(bf16[12,32,1024]{2,1,0:T(8,128)(2,1)} %param.11) | copy-start | bytes 2359300
  92.1 50.2 %all-to-all-start = ((bf16[32,2,12288]{2,1,0:T(2,128)(2,1)}), bf16[32,2,12288]{2,1,0:T(2,128)(2,1)}, u32[]{:S(2)}, u32[]{:S(2)}) async-start(bf16[32,2,12288]{2,1,0:T(2,128)(2,1)} %reshape.94), calls=%async_computation | async-start | bytes 3145728 | tf_op jit(solution)/shard_map/all_to_all | solution.py:75
  104.4 424.3 %all-gather.3.cloned.1.call-start = ((), (), s32[]{:S(2)}) async-start(), calls=%async_computation.4 | async-start | bytes 8421376 | tf_op jit(solution)/shard_map/all_gather | solution.py:114
  175.8 18.3 %copy-start.4 = (bf16[12,2,1024,32]{2,3,1,0:T(8,128)(2,1)S(1)}, bf16[12,2,1024,32]{2,3,1,0:T(8,128)(2,1)}, u32[]{:S(2)}) copy-start(bf16[12,2,1024,32]{2,3,1,0:T(8,128)(2,1)} %all_to_all.29) | copy-start | bytes 4718596
  211.5 1.4 copy-start.3
  353.7 18.3 %copy-start.5 = (bf16[12,2,1024,32]{2,3,1,0:T(8,128)(2,1)S(1)}, bf16[12,2,1024,32]{2,3,1,0:T(8,128)(2,1)}, u32[]{:S(2)}) copy-start(bf16[12,2,1024,32]{2,3,1,0:T(8,128)(2,1)} %all_to_all.33) | copy-start | bytes 4718596
  390.1 11.4 %copy-start.2 = (bf16[64,32,1024]{2,1,0:T(8,128)(2,1)S(1)}, bf16[64,32,1024]{2,1,0:T(8,128)(2,1)}, u32[]{:S(2)}) copy-start(bf16[64,32,1024]{2,1,0:T(8,128)(2,1)} %param.6) | copy-start | bytes 12582916
  407.0 126.3 %reduce-scatter.2.cloned.1.call-start = ((), (), s32[]{:S(2)}) async-start(), calls=%async_computation.3 | async-start | bytes 9437184 | tf_op jit(solution)/shard_map/reduce_scatter | solution.py:116
  528.7 7.4 %copy-start.1 = (bf16[64,64]{1,0:T(8,128)(2,1)S(1)}, bf16[64,64]{1,0:T(8,128)(2,1)}, u32[]{:S(2)}) copy-start(bf16[64,64]{1,0:T(8,128)(2,1)} %param.7) | copy-start | bytes 24580
Sparse Core Ops, SparseCore 0:
  407.2 121.5 all-gather.2
Sparse Core Ops, SparseCore 1:
  412.9 55.5 reduce-scatter.1
